TPU v7x, 32 devices: a whole 2x2x4 slice. The times are simulated.
32 devices in a mesh: section: 4 (over y, x), expert: 8 (over z, core).
Axes of the slice: x: 2, y: 2, z: 4, core: 2. Of those that a mesh axis runs over, the one named last changes fastest.
Arguments:
- forward_input: bfloat16 [4, 576, 4096], P('section', 'expert'), may hold values from -6 to 6
- backward_cotangent: bfloat16 [4, 576, 4096], P('section', 'expert'), may hold values from -6 to 6
- saved_input: bfloat16 [4, 576, 4096], P('section', 'expert'), may hold values from -6 to 6
- saved_hidden: bfloat16 [4, 8, 360, 1536], P('section', 'expert'), may hold values from -8 to 8
- norm_gain: float32 [4, 4096], P('section'), may hold values from 0.5 to 2
- forward_experts: int32 [4, 576, 4], P('section', 'expert'), may hold values from 0 to 7, all different within a row; in each aligned block of 72 rows (0 to 71, 72 to 143, ..., all dimensions but the last counted through in order) at most 45 rows name the same one
- forward_gates: float32 [4, 576, 4], P('section', 'expert'), may hold values from 0.05 to 1
- backward_experts: int32 [4, 576, 4], P('section', 'expert'), may hold values from 0 to 7, all different within a row; in each aligned block of 72 rows (0 to 71, 72 to 143, ..., all dimensions but the last counted through in order) at most 45 rows name the same one
- backward_gates: float32 [4, 576, 4], P('section', 'expert'), may hold values from 0.05 to 1
- gate_up_weight: bfloat16 [4, 8, 4096, 1536], P('section', 'expert'), may hold values from -0.09375 to 0.09375
- down_weight: bfloat16 [4, 8, 768, 4096], P('section', 'expert'), may hold values from -0.21875 to 0.21875
Outputs:
- forward_output: bfloat16 [4, 576, 4096], P('section', 'expert')
- input_gradient: bfloat16 [4, 576, 4096], P('section', 'expert')
Inputs may be any that keep to these rules, and one draw needn't show every extreme that they name: `forward_experts`: each token names 4 distinct experts. In the rows of one device (aligned blocks of 72 tokens) no expert is named by more than 45 entries, and in some device's rows some expert is named by exactly 45. `backward_experts`: same law as forward_experts, drawn independently.
All inputs are finite; a program needn't handle non-finite values.
Results may differ from a plain program's by a relative error of at most 0.0054.
Values may be sent and summed in bfloat16 or wider, within the bound.
A program may use at most 128 MiB of HBM per device.

v0:
```python
import jax
import jax.numpy as jnp
from jax import lax
from jax.sharding import PartitionSpec as P

EPSILON = 1e-06


def passed_along(value, axis, steps):
    count = lax.axis_size(axis)
    initial, last = (max(0, -steps), min(count, count - steps))
    return lax.ppermute(value, axis, [(source, source + steps) for source in range(initial, last)])


def norm_scale(values, gain_row):
    widened = values.astype(jnp.float32)
    inverse = lax.rsqrt(jnp.mean(widened * widened, axis=-1, keepdims=True) + EPSILON)
    return widened * inverse * gain_row


def dense_weights(expert_ids, gates, expert_count):
    weights = gates / jnp.sum(gates, axis=-1, keepdims=True)
    onehot = expert_ids[:, :, None] == jnp.arange(expert_count, dtype=jnp.int32)[None, None, :]
    return jnp.sum(jnp.where(onehot, weights[:, :, None], 0.0), axis=1)


def local(
    forward_input,
    backward_cotangent,
    saved_input,
    saved_hidden,
    norm_gain,
    forward_experts,
    forward_gates,
    backward_experts,
    backward_gates,
    gate_up_weight,
    down_weight,
):
    peer_count = lax.axis_size("expert")
    me = lax.axis_index("expert")
    table = jnp.concatenate(
        [
            dense_weights(forward_experts[0], forward_gates[0], peer_count),
            dense_weights(backward_experts[0], backward_gates[0], peer_count),
        ],
        axis=1,
    )
    tables = lax.all_gather(table, "expert", axis=0, tiled=True)
    weight_f = lax.dynamic_slice_in_dim(tables, me, 1, axis=1)
    weight_b = lax.dynamic_slice_in_dim(tables, peer_count + me, 1, axis=1)
    moved_input, moved_cotangent = passed_along((forward_input, backward_cotangent), "section", 1)
    is_first = lax.axis_index("section") == 0
    layer_in = jnp.where(is_first, forward_input, moved_input)[0]
    cotangent = jnp.where(is_first, backward_cotangent, moved_cotangent)[0]
    token_count = layer_in.shape[0]
    slot_total = saved_hidden.shape[2]
    capacity = slot_total // peer_count
    gain_row = norm_gain[0]
    weight_in = gate_up_weight[0, 0]
    weight_down = down_weight[0, 0]
    hidden_width = weight_down.shape[0]
    normed = norm_scale(layer_in, gain_row).astype(jnp.bfloat16)
    all_normed = lax.all_gather(normed, "expert", axis=0, tiled=True)
    all_cotangent = lax.all_gather(cotangent, "expert", axis=0, tiled=True)
    projected = jnp.dot(all_normed, weight_in, preferred_element_type=jnp.float32)
    hidden = (jax.nn.silu(projected[:, :hidden_width]) * projected[:, hidden_width:]).astype(
        jnp.bfloat16
    )
    served = jnp.dot(hidden, weight_down, preferred_element_type=jnp.float32)
    served = (served * weight_f).astype(jnp.bfloat16)
    mixture = lax.psum_scatter(served, "expert", scatter_dimension=0, tiled=True)
    forward_output = (layer_in.astype(jnp.float32) + mixture.astype(jnp.float32)).astype(
        jnp.bfloat16
    )
    routed = (weight_b > 0.0).reshape(peer_count, token_count)
    slot = jnp.cumsum(routed.astype(jnp.int32), axis=1) - 1
    spread = (
        (slot[:, :, None] == jnp.arange(capacity, dtype=jnp.int32)[None, None, :])
        & routed[:, :, None]
    ).astype(jnp.bfloat16)
    saved = jnp.einsum(
        "jts,jsf->jtf",
        spread,
        saved_hidden[0, 0].reshape(peer_count, capacity, -1),
        preferred_element_type=jnp.float32,
    ).reshape(peer_count * token_count, -1)
    scaled = (weight_b * all_cotangent.astype(jnp.float32)).astype(jnp.bfloat16)
    grad_hidden = lax.dot_general(
        scaled, weight_down, (((1,), (1,)), ((), ())), preferred_element_type=jnp.float32
    )
    gate, up = (saved[:, :hidden_width], saved[:, hidden_width:])
    sig = jax.nn.sigmoid(gate)
    grad_both = jnp.concatenate(
        [grad_hidden * up * sig * (1.0 + gate * (1.0 - sig)), grad_hidden * gate * sig], axis=1
    ).astype(jnp.bfloat16)
    grads = lax.dot_general(
        grad_both, weight_in, (((1,), (1,)), ((), ())), preferred_element_type=jnp.float32
    ).astype(jnp.bfloat16)
    grad_normed = lax.psum_scatter(grads, "expert", scatter_dimension=0, tiled=True).astype(
        jnp.float32
    )

    def apply_norm(inputs):
        return norm_scale(inputs, gain_row)

    primal, pullback = jax.vjp(apply_norm, saved_input[0].astype(jnp.float32))
    input_gradient = (cotangent.astype(jnp.float32) + pullback(grad_normed)[0]).astype(jnp.bfloat16)
    return (forward_output[None], input_gradient[None])


def solution(mesh):
    row = P("section", "expert", None)
    block = P("section", "expert", None, None)
    in_specs = (row, row, row, block, P("section", None), row, row, row, row, block, block)
    return jax.shard_map(local, mesh=mesh, in_specs=in_specs, out_specs=(row, row), check_vma=False)
```

profile of v0, /device:TPU:0, one launch (start us, length us, event | category | flops | bytes accessed | tf_op | source)
XLA Modules:
  0.0 298.4 jit_solution(10791374151857974960)
XLA Ops:
  7.3 5.0 %collective-permute-start.1 = (bf16[1,72,4096]{2,1,0:T(8,128)(2,1)}, bf16[1,72,4096]{2,1,0:T(8,128)(2,1)S(1)}, u32[]{:S(2)}, u32[]{:S(2)}) collective-permute-start(bf16[1,72,4096]{2,1,0:T(8,128)(2,1)} %param.12), channel_id=1, source_target_pairs={{0,8},{8,16},{16,24},{1,9},{9,17},{17,25},{2,10},{10,18},{18,26},{... | collective-permute-start | bytes 1769480 | tf_op jit(solution)/shard_map/ppermute | solution.py:12
  12.3 12.8 %collective-permute-done.1 = bf16[1,72,4096]{2,1,0:T(8,128)(2,1)S(1)} collective-permute-done((bf16[1,72,4096]{2,1,0:T(8,128)(2,1)}, bf16[1,72,4096]{2,1,0:T(8,128)(2,1)S(1)}, u32[]{:S(2)}, u32[]{:S(2)}) %collective-permute-start.1) | collective-permute-done | bytes 589856 | tf_op jit(solution)/shard_map/ppermute | solution.py:12
  25.1 2.0 broadcast_select_fusion
  27.3 14.3 %all-gather.1 = f32[8,72,16]{1,2,0:T(8,128)S(1)} all-gather(f32[1,72,16]{1,2,0:T(8,128)S(1)} %maximum_bitcast_fusion), channel_id=1, replica_groups=mesh['section'=4,'expert'=8] {'expert'}, dimensions={0}, use_global_device_ids=true | all-gather | bytes 41472 | tf_op jit(solution)/shard_map/all_gather | solution.py:49
  41.7 0.3 reshape_squeeze.3
  42.1 0.1 reshape.92
  42.2 0.2 reduce_window_sum.11
  42.5 2.4 fusion.34
  44.9 35.2 %all-gather.7.cloned.1.call-done = bf16[1,576,4096]{2,1,0:T(8,128)(2,1)} async-done(((bf16[1,72,4096]{2,1,0:T(8,128)(2,1)}), bf16[1,576,4096]{2,1,0:T(8,128)(2,1)}) %all-gather.7.cloned.1.call-update) | async-done | bytes 4718608 | tf_op jit(solution)/shard_map/all_gather | solution.py:65
  80.1 9.4 %fusion.16 = (bf16[576,768]{1,0:T(8,128)(2,1)S(1)}, bf16[576,768]{1,0:T(8,128)(2,1)S(1)}) fusion(f32[576,1536]{1,0:T(8,128)} %bitcast.55, bf16[1,1,768,4096]{3,2,1,0:T(8,128)(2,1)} %param.21, bf16[1,576,4096]{2,1,0:T(8,128)(2,1)} %all-gather.7.cloned.1.call-done, f32[576]{0:T(1024)S(1)} %get-tuple-element.4), kind=kOutput, calls=%fused_computation.16 | convolution fusion | flops 3636707328 | bytes 16320768 | tf_op jit(solution)/shard_map/dot_general | solution.py:89
  89.6 18.4 %fusion.8 = bf16[576,4096]{1,0:T(8,128)(2,1)} fusion(bf16[1,1,4096,1536]{3,2,1,0:T(8,128)(2,1)} %param.20, bf16[576,768]{1,0:T(8,128)(2,1)S(1)} %get-tuple-element.9, bf16[576,768]{1,0:T(8,128)(2,1)S(1)} %get-tuple-element.8), kind=kOutput, calls=%fused_computation.10 | convolution fusion | flops 7253655552 | bytes 19070976 | tf_op jit(solution)/shard_map/dot_general | solution.py:97
  108.0 1.0 copy-done.3
  109.0 3.4 %collective-permute-start = (bf16[1,72,4096]{2,1,0:T(8,128)(2,1)S(1)}, bf16[1,72,4096]{2,1,0:T(8,128)(2,1)S(1)}, u32[]{:S(2)}, u32[]{:S(2)}) collective-permute-start(bf16[1,72,4096]{2,1,0:T(8,128)(2,1)S(1)} %copy-done.3), channel_id=1, source_target_pairs={{0,8},{8,16},{16,24},{1,9},{9,17},{17,25},{2,10},{10,18},{18,26},{... | collective-permute-start | bytes 1769480 | tf_op jit(solution)/shard_map/ppermute | solution.py:12
  112.4 12.9 %collective-permute-done = bf16[1,72,4096]{2,1,0:T(8,128)(2,1)S(1)} collective-permute-done((bf16[1,72,4096]{2,1,0:T(8,128)(2,1)S(1)}, bf16[1,72,4096]{2,1,0:T(8,128)(2,1)S(1)}, u32[]{:S(2)}, u32[]{:S(2)}) %collective-permute-start) | collective-permute-done | bytes 589856 | tf_op jit(solution)/shard_map/ppermute | solution.py:12
  125.3 0.3 fusion.23
  125.6 36.1 %reduce-scatter.5.cloned.1.call-done = bf16[72,4096]{1,0:T(8,128)(2,1)} async-done(((bf16[576,4096]{1,0:T(8,128)(2,1)}), bf16[72,4096]{1,0:T(8,128)(2,1)}) %reduce-scatter.5.cloned.1.call-update) | async-done | bytes 589840 | tf_op jit(solution)/shard_map/reduce_scatter | solution.py:100
  161.7 1.4 fusion.27
  163.2 2.6 fusion.32
  165.9 0.2 reduce-scatter.3.cloned.1.call-start
  166.1 50.0 %all-gather.5.cloned.1.call-done = bf16[576,4096]{1,0:T(8,128)(2,1)} async-done(((bf16[72,4096]{1,0:T(8,128)(2,1)}), bf16[576,4096]{1,0:T(8,128)(2,1)}) %all-gather.5.cloned.1.call-update) | async-done | bytes 4718608 | tf_op jit(solution)/shard_map/all_gather | solution.py:64
  216.1 11.5 %fusion.2 = f32[576,1536]{1,0:T(8,128)S(1)} fusion(bf16[576,4096]{1,0:T(8,128)(2,1)} %all-gather.5.cloned.1.call-done, bf16[1,1,4096,1536]{3,2,1,0:T(8,128)(2,1)} %param.20), kind=kOutput, calls=%fused_computation.2 | convolution fusion | flops 7247757312 | bytes 20840448 | tf_op jit(solution)/shard_map/dot_general | solution.py:66
  227.5 8.4 %multiply_convert_fusion = bf16[576,4096]{1,0:T(8,128)(2,1)} fusion(bf16[1,1,768,4096]{3,2,1,0:T(8,128)(2,1)} %param.21, f32[576]{0:T(1024)S(1)} %get-tuple-element.5, f32[576,1536]{1,0:T(8,128)S(1)} %fusion.2), kind=kOutput, calls=%fused_computation.6 | convolution fusion | flops 3631251456 | bytes 14551296 | tf_op jit(solution)/shard_map/dot_general | solution.py:70
  235.9 53.9 %reduce-scatter.3.cloned.1.call-done = bf16[72,4096]{1,0:T(8,128)(2,1)} async-done(((bf16[576,4096]{1,0:T(8,128)(2,1)}), bf16[72,4096]{1,0:T(8,128)(2,1)}) %reduce-scatter.3.cloned.1.call-update) | async-done | bytes 589840 | tf_op jit(solution)/shard_map/reduce_scatter | solution.py:72
  289.9 2.0 fusion.31
  (38 shorter events, 0.5 us)
Async XLA Ops:
  7.2 20.0 %copy-start.5 = (f32[1,72,4]{1,2,0:T(4,128)S(1)}, f32[1,72,4]{1,2,0:T(4,128)}, u32[]{:S(2)}) copy-start(f32[1,72,4]{1,2,0:T(4,128)} %param.19) | copy-start | bytes 3460
  7.2 20.0 %copy-start.6 = (f32[1,72,4]{1,2,0:T(4,128)S(1)}, f32[1,72,4]{1,2,0:T(4,128)}, u32[]{:S(2)}) copy-start(f32[1,72,4]{1,2,0:T(4,128)} %param.17) | copy-start | bytes 3460
  7.2 20.1 %copy-start.7 = (s32[1,72,4]{1,2,0:T(4,128)S(1)}, s32[1,72,4]{1,2,0:T(4,128)}, u32[]{:S(2)}) copy-start(s32[1,72,4]{1,2,0:T(4,128)} %param.18) | copy-start | bytes 3460
  7.2 20.1 %copy-start.8 = (s32[1,72,4]{1,2,0:T(4,128)S(1)}, s32[1,72,4]{1,2,0:T(4,128)}, u32[]{:S(2)}) copy-start(s32[1,72,4]{1,2,0:T(4,128)} %param.16) | copy-start | bytes 3460
  7.2 34.5 %copy-start.2 = (bf16[1,1,360,1536]{3,2,1,0:T(8,128)(2,1)S(1)}, bf16[1,1,360,1536]{3,2,1,0:T(8,128)(2,1)}, u32[]{:S(2)}) copy-start(bf16[1,1,360,1536]{3,2,1,0:T(8,128)(2,1)} %param.14) | copy-start | bytes 3317764
  7.2 72.9 %all-gather.7.cloned.1.call-start = ((), (), s32[]{:S(2)}) async-start(), calls=%async_computation.5 | async-start | bytes 5308416 | tf_op jit(solution)/shard_map/all_gather | solution.py:65
  7.3 17.9 %collective-permute-start.1 = (bf16[1,72,4096]{2,1,0:T(8,128)(2,1)}, bf16[1,72,4096]{2,1,0:T(8,128)(2,1)S(1)}, u32[]{:S(2)}, u32[]{:S(2)}) collective-permute-start(bf16[1,72,4096]{2,1,0:T(8,128)(2,1)} %param.12), channel_id=1, source_target_pairs={{0,8},{8,16},{16,24},{1,9},{9,17},{17,25},{2,10},{10,18},{18,26},{... | collective-permute-start | bytes 1769480 | tf_op jit(solution)/shard_map/ppermute | solution.py:12
  27.1 134.6 %reduce-scatter.5.cloned.1.call-start = ((), (), s32[]{:S(2)}) async-start(), calls=%async_computation.4 | async-start | bytes 5308416 | tf_op jit(solution)/shard_map/reduce_scatter | solution.py:100
  107.9 1.1 copy-start.3
  107.9 53.8 %copy-start.1 = (bf16[1,72,4096]{2,1,0:T(8,128)(2,1)S(1)}, bf16[1,72,4096]{2,1,0:T(8,128)(2,1)}, u32[]{:S(2)}) copy-start(bf16[1,72,4096]{2,1,0:T(8,128)(2,1)} %param.13) | copy-start | bytes 1769476
  107.9 53.8 %copy-start.4 = (f32[1,4096]{1,0:T(1,128)S(1)}, f32[1,4096]{1,0:T(1,128)}, u32[]{:S(2)}) copy-start(f32[1,4096]{1,0:T(1,128)} %param.15) | copy-start | bytes 49156
  108.0 55.2 %copy-start = (bf16[1,72,4096]{2,1,0:T(8,128)(2,1)S(1)}, bf16[1,72,4096]{2,1,0:T(8,128)(2,1)}, u32[]{:S(2)}) copy-start(bf16[1,72,4096]{2,1,0:T(8,128)(2,1)} %broadcast_select_fusion) | copy-start | bytes 1769476
  108.0 108.1 %all-gather.5.cloned.1.call-start = ((), (), s32[]{:S(2)}) async-start(), calls=%async_computation.2 | async-start | bytes 5308416 | tf_op jit(solution)/shard_map/all_gather | solution.py:64
  109.0 16.3 %collective-permute-start = (bf16[1,72,4096]{2,1,0:T(8,128)(2,1)S(1)}, bf16[1,72,4096]{2,1,0:T(8,128)(2,1)S(1)}, u32[]{:S(2)}, u32[]{:S(2)}) collective-permute-start(bf16[1,72,4096]{2,1,0:T(8,128)(2,1)S(1)} %copy-done.3), channel_id=1, source_target_pairs={{0,8},{8,16},{16,24},{1,9},{9,17},{17,25},{2,10},{10,18},{18,26},{... | collective-permute-start | bytes 1769480 | tf_op jit(solution)/shard_map/ppermute | solution.py:12
  165.9 124.0 %reduce-scatter.3.cloned.1.call-start = ((), (), s32[]{:S(2)}) async-start(), calls=%async_computation.3 | async-start | bytes 5308416 | tf_op jit(solution)/shard_map/reduce_scatter | solution.py:72
Sparse Core Ops, SparseCore 0:
  27.2 52.8 all-gather.6
  108.1 53.6 reduce-scatter.4
  166.0 50.0 all-gather.4
  236.1 53.7 reduce-scatter.2
where the time goes:
time: 299 us; the launch traced here: 298 us
  waiting for transfers between devices  201 us (67%)
  matrix products  50 us (17%)
  blocking collectives  14.3 us (5%)
  between operations  14 us (5%)
  starting transfers between devices  8.75 us (3%)
  other arithmetic  8.72 us (3%)
    reduce_scatter x1, waiting for transfers between devices, local(): lax.psum_scatter(served, 'expert', scatter_dimension=0, tiled=True)  53.9 us
    all_gather x1, waiting for transfers between devices, local(): all_normed = lax.all_gather(normed, 'expert', axis=0, tiled=True)  50 us
    reduce_scatter x1, waiting for transfers between devices, local(): lax.psum_scatter(grads, 'expert', scatter_dimension=0, tiled=True)  36.1 us
    all_gather x1, waiting for transfers between devices, local(): all_cotangent = lax.all_gather(cotangent, 'expert', axis=0, tiled=True)  35.2 us
    ppermute x2, waiting for transfers between devices, passed_along(): lax.ppermute(value, axis, [(source, source + steps) for source in range(i...  25.8 us
    dot_general x1, matrix products, local(): lax.dot_general(grad_both, weight_in, (((1,), (1,)), ((), ())), preferred...  18.4 us
    all_gather x1, blocking collectives, local(): tables = lax.all_gather(table, 'expert', axis=0, tiled=True)  14.3 us
    dot_general x1, matrix products, local(): jnp.dot(all_normed, weight_in, preferred_element_type=jnp.float32)  11.5 us
  transfers between devices with their start and end apart: 6, of which 6 were waited for; matrix products, arithmetic and copies ran while one was open for 1% of the time, Pallas kernels for 0%

commit v1 on v0

--- a/solution.py
+++ b/solution.py
@@ -46,7 +46,14 @@
         ],
         axis=1,
     )
-    tables = lax.all_gather(table, "expert", axis=0, tiled=True)
+    ring = [table]
+    for hop in range(7):
+        ring.append(lax.ppermute(ring[-1], "expert", [(dev, (dev + 1) % 8) for dev in range(8)]))
+    tables = jnp.roll(
+        jnp.concatenate(ring[::-1], axis=0),
+        (lax.axis_index("expert") + 1) * ring[0].shape[0],
+        axis=0,
+    )
     weight_f = lax.dynamic_slice_in_dim(tables, me, 1, axis=1)
     weight_b = lax.dynamic_slice_in_dim(tables, peer_count + me, 1, axis=1)
     moved_input, moved_cotangent = passed_along((forward_input, backward_cotangent), "section", 1)

time: 299 us -> 299 us (level)
  waiting for transfers between devices: 201 us -> 216 us
  blocking collectives: 14.3 us -> 0 us
    ppermute x0 -> x7, waiting for transfers between devices: none -> 34.7 us  [local(): lax.ppermute(ring[-1], 'expert', [(dev, (dev + 1) % 8) for dev in range(8)])]
    all_gather x1, waiting for transfers between devices: 35.2 us -> 14.9 us  [local(): all_cotangent = lax.all_gather(cotangent, 'expert', axis=0, tiled=True)]
    all_gather x1 -> x0, blocking collectives: 14.3 us -> none  [local(): tables = lax.all_gather(table, 'expert', axis=0, tiled=True)]
  transfers between devices with their start and end apart: 6 -> 13, of which waited for: 6 -> 13; matrix products, arithmetic and copies ran while one was open for 1% -> 1% of each run, Pallas kernels for 0% -> 0%
where the time goes in v1:
time: 299 us
  waiting for transfers between devices  216 us (72%)
  matrix products  50 us (17%)
  between operations  14 us (5%)
  starting transfers between devices  8.79 us (3%)
  other arithmetic  8.79 us (3%)
    reduce_scatter x1, waiting for transfers between devices, local(): lax.psum_scatter(served, 'expert', scatter_dimension=0, tiled=True)  53.9 us
    all_gather x1, waiting for transfers between devices, local(): all_normed = lax.all_gather(normed, 'expert', axis=0, tiled=True)  50 us
    reduce_scatter x1, waiting for transfers between devices, local(): lax.psum_scatter(grads, 'expert', scatter_dimension=0, tiled=True)  36.3 us
    ppermute x7, waiting for transfers between devices, local(): lax.ppermute(ring[-1], 'expert', [(dev, (dev + 1) % 8) for dev in range(8)])  34.7 us
    ppermute x2, waiting for transfers between devices, passed_along(): lax.ppermute(value, axis, [(source, source + steps) for source in range(i...  25.8 us
    dot_general x1, matrix products, local(): lax.dot_general(grad_both, weight_in, (((1,), (1,)), ((), ())), preferred...  18.4 us
    all_gather x1, waiting for transfers between devices, local(): all_cotangent = lax.all_gather(cotangent, 'expert', axis=0, tiled=True)  14.9 us
    dot_general x1, matrix products, local(): jnp.dot(all_normed, weight_in, preferred_element_type=jnp.float32)  11.5 us
  transfers between devices with their start and end apart: 13, of which 13 were waited for; matrix products, arithmetic and copies ran while one was open for 1% of the time, Pallas kernels for 0%

profile of v1, /device:TPU:0, one launch (start us, length us, event | category | flops | bytes accessed | tf_op | source)
XLA Modules:
  0.0 298.8 jit_solution(8016240804026072334)
XLA Ops:
  7.3 5.0 %collective-permute-start.8 = (bf16[1,72,4096]{2,1,0:T(8,128)(2,1)}, bf16[1,72,4096]{2,1,0:T(8,128)(2,1)S(1)}, u32[]{:S(2)}, u32[]{:S(2)}) collective-permute-start(bf16[1,72,4096]{2,1,0:T(8,128)(2,1)} %param.12), channel_id=1, source_target_pairs={{0,8},{8,16},{16,24},{1,9},{9,17},{17,25},{2,10},{10,18},{18,26},{... | collective-permute-start | bytes 1769480 | tf_op jit(solution)/shard_map/ppermute | solution.py:12
  12.3 12.8 %collective-permute-done.8 = bf16[1,72,4096]{2,1,0:T(8,128)(2,1)S(1)} collective-permute-done((bf16[1,72,4096]{2,1,0:T(8,128)(2,1)}, bf16[1,72,4096]{2,1,0:T(8,128)(2,1)S(1)}, u32[]{:S(2)}, u32[]{:S(2)}) %collective-permute-start.8) | collective-permute-done | bytes 589856 | tf_op jit(solution)/shard_map/ppermute | solution.py:12
  25.1 2.0 broadcast_select_fusion
  27.4 4.9 %collective-permute-done.1 = f32[72,16]{0,1:T(8,128)S(1)} collective-permute-done((f32[72,16]{0,1:T(8,128)S(1)}, f32[72,16]{0,1:T(8,128)S(1)}, u32[]{:S(2)}, u32[]{:S(2)}) %collective-permute-start.1) | collective-permute-done | bytes 4640 | tf_op jit(solution)/shard_map/ppermute | solution.py:51
  32.2 4.9 %collective-permute-done.2 = f32[72,16]{0,1:T(8,128)S(1)} collective-permute-done((f32[72,16]{0,1:T(8,128)S(1)}, f32[72,16]{0,1:T(8,128)S(1)}, u32[]{:S(2)}, u32[]{:S(2)}) %collective-permute-start.2) | collective-permute-done | bytes 4640 | tf_op jit(solution)/shard_map/ppermute | solution.py:51
  37.1 5.0 %collective-permute-done.3 = f32[72,16]{0,1:T(8,128)S(1)} collective-permute-done((f32[72,16]{0,1:T(8,128)S(1)}, f32[72,16]{0,1:T(8,128)S(1)}, u32[]{:S(2)}, u32[]{:S(2)}) %collective-permute-start.3) | collective-permute-done | bytes 4640 | tf_op jit(solution)/shard_map/ppermute | solution.py:51
  42.1 5.0 %collective-permute-done.4 = f32[72,16]{0,1:T(8,128)S(1)} collective-permute-done((f32[72,16]{0,1:T(8,128)S(1)}, f32[72,16]{0,1:T(8,128)S(1)}, u32[]{:S(2)}, u32[]{:S(2)}) %collective-permute-start.4) | collective-permute-done | bytes 4640 | tf_op jit(solution)/shard_map/ppermute | solution.py:51
  47.2 5.0 %collective-permute-done.5 = f32[72,16]{0,1:T(8,128)S(1)} collective-permute-done((f32[72,16]{0,1:T(8,128)S(1)}, f32[72,16]{0,1:T(8,128)S(1)}, u32[]{:S(2)}, u32[]{:S(2)}) %collective-permute-start.5) | collective-permute-done | bytes 4640 | tf_op jit(solution)/shard_map/ppermute | solution.py:51
  52.2 5.1 %collective-permute-done.6 = f32[72,16]{0,1:T(8,128)S(1)} collective-permute-done((f32[72,16]{0,1:T(8,128)S(1)}, f32[72,16]{0,1:T(8,128)S(1)}, u32[]{:S(2)}, u32[]{:S(2)}) %collective-permute-start.6) | collective-permute-done | bytes 4640 | tf_op jit(solution)/shard_map/ppermute | solution.py:51
  57.6 4.8 %collective-permute-done.7 = f32[72,16]{0,1:T(8,128)S(1)} collective-permute-done((f32[72,16]{0,1:T(8,128)S(1)}, f32[72,16]{0,1:T(8,128)S(1)}, u32[]{:S(2)}, u32[]{:S(2)}) %collective-permute-start.7) | collective-permute-done | bytes 4640 | tf_op jit(solution)/shard_map/ppermute | solution.py:51
  63.1 2.4 fusion.39
  65.5 14.9 %all-gather.6.cloned.1.call-done = bf16[1,576,4096]{2,1,0:T(8,128)(2,1)} async-done(((bf16[1,72,4096]{2,1,0:T(8,128)(2,1)}), bf16[1,576,4096]{2,1,0:T(8,128)(2,1)}) %all-gather.6.cloned.1.call-update) | async-done | bytes 4718608 | tf_op jit(solution)/shard_map/all_gather | solution.py:72
  80.4 9.4 %fusion.17 = (bf16[576,768]{1,0:T(8,128)(2,1)S(1)}, bf16[576,768]{1,0:T(8,128)(2,1)S(1)}) fusion(f32[576,1536]{1,0:T(8,128)} %bitcast.53, bf16[1,1,768,4096]{3,2,1,0:T(8,128)(2,1)} %param.21, bf16[1,576,4096]{2,1,0:T(8,128)(2,1)} %all-gather.6.cloned.1.call-done, f32[576]{0:T(1024)S(1)} %get-tuple-element.4), kind=kOutput, calls=%fused_computation.17 | convolution fusion | flops 3636707328 | bytes 16320768 | tf_op jit(solution)/shard_map/dot_general | solution.py:96
  89.8 18.4 %fusion.9 = bf16[576,4096]{1,0:T(8,128)(2,1)} fusion(bf16[1,1,4096,1536]{3,2,1,0:T(8,128)(2,1)} %param.20, bf16[576,768]{1,0:T(8,128)(2,1)S(1)} %get-tuple-element.9, bf16[576,768]{1,0:T(8,128)(2,1)S(1)} %get-tuple-element.8), kind=kOutput, calls=%fused_computation.11 | convolution fusion | flops 7253655552 | bytes 19070976 | tf_op jit(solution)/shard_map/dot_general | solution.py:104
  109.2 3.4 %collective-permute-start = (bf16[1,72,4096]{2,1,0:T(8,128)(2,1)S(1)}, bf16[1,72,4096]{2,1,0:T(8,128)(2,1)S(1)}, u32[]{:S(2)}, u32[]{:S(2)}) collective-permute-start(bf16[1,72,4096]{2,1,0:T(8,128)(2,1)S(1)} %copy-done.3), channel_id=1, source_target_pairs={{0,8},{8,16},{16,24},{1,9},{9,17},{17,25},{2,10},{10,18},{18,26},{... | collective-permute-start | bytes 1769480 | tf_op jit(solution)/shard_map/ppermute | solution.py:12
  112.6 12.9 %collective-permute-done = bf16[1,72,4096]{2,1,0:T(8,128)(2,1)S(1)} collective-permute-done((bf16[1,72,4096]{2,1,0:T(8,128)(2,1)S(1)}, bf16[1,72,4096]{2,1,0:T(8,128)(2,1)S(1)}, u32[]{:S(2)}, u32[]{:S(2)}) %collective-permute-start) | collective-permute-done | bytes 589856 | tf_op jit(solution)/shard_map/ppermute | solution.py:12
  125.9 36.3 %reduce-scatter.5.cloned.1.call-done = bf16[72,4096]{1,0:T(8,128)(2,1)} async-done(((bf16[576,4096]{1,0:T(8,128)(2,1)}), bf16[72,4096]{1,0:T(8,128)(2,1)}) %reduce-scatter.5.cloned.1.call-update) | async-done | bytes 589840 | tf_op jit(solution)/shard_map/reduce_scatter | solution.py:107
  162.1 1.4 fusion.28
  163.6 2.6 fusion.37
  166.5 50.0 %all-gather.4.cloned.1.call-done = bf16[576,4096]{1,0:T(8,128)(2,1)} async-done(((bf16[72,4096]{1,0:T(8,128)(2,1)}), bf16[576,4096]{1,0:T(8,128)(2,1)}) %all-gather.4.cloned.1.call-update) | async-done | bytes 4718608 | tf_op jit(solution)/shard_map/all_gather | solution.py:71
  216.5 11.5 %fusion.2 = f32[576,1536]{1,0:T(8,128)S(1)} fusion(bf16[576,4096]{1,0:T(8,128)(2,1)} %all-gather.4.cloned.1.call-done, bf16[1,1,4096,1536]{3,2,1,0:T(8,128)(2,1)} %param.20), kind=kOutput, calls=%fused_computation.2 | convolution fusion | flops 7247757312 | bytes 20840448 | tf_op jit(solution)/shard_map/dot_general | solution.py:73
  227.9 8.4 %multiply_convert_fusion = bf16[576,4096]{1,0:T(8,128)(2,1)} fusion(f32[576]{0:T(1024)S(1)} %get-tuple-element.5, bf16[1,1,768,4096]{3,2,1,0:T(8,128)(2,1)} %param.21, f32[576,1536]{1,0:T(8,128)S(1)} %fusion.2), kind=kOutput, calls=%fused_computation.6 | convolution fusion | flops 3631251456 | bytes 14551296 | tf_op jit(solution)/shard_map/dot_general | solution.py:77
  236.3 53.9 %reduce-scatter.3.cloned.1.call-done = bf16[72,4096]{1,0:T(8,128)(2,1)} async-done(((bf16[576,4096]{1,0:T(8,128)(2,1)}), bf16[72,4096]{1,0:T(8,128)(2,1)}) %reduce-scatter.3.cloned.1.call-update) | async-done | bytes 589840 | tf_op jit(solution)/shard_map/reduce_scatter | solution.py:79
  290.3 2.0 fusion.36
  (50 shorter events, 2.8 us)
Async XLA Ops:
  7.2 20.0 %copy-start.5 = (f32[1,72,4]{1,2,0:T(4,128)S(1)}, f32[1,72,4]{1,2,0:T(4,128)}, u32[]{:S(2)}) copy-start(f32[1,72,4]{1,2,0:T(4,128)} %param.19) | copy-start | bytes 3460
  7.2 20.0 %copy-start.6 = (f32[1,72,4]{1,2,0:T(4,128)S(1)}, f32[1,72,4]{1,2,0:T(4,128)}, u32[]{:S(2)}) copy-start(f32[1,72,4]{1,2,0:T(4,128)} %param.17) | copy-start | bytes 3460
  7.2 20.1 %copy-start.7 = (s32[1,72,4]{1,2,0:T(4,128)S(1)}, s32[1,72,4]{1,2,0:T(4,128)}, u32[]{:S(2)}) copy-start(s32[1,72,4]{1,2,0:T(4,128)} %param.18) | copy-start | bytes 3460
  7.2 20.1 %copy-start.8 = (s32[1,72,4]{1,2,0:T(4,128)S(1)}, s32[1,72,4]{1,2,0:T(4,128)}, u32[]{:S(2)}) copy-start(s32[1,72,4]{1,2,0:T(4,128)} %param.16) | copy-start | bytes 3460
  7.2 50.1 %copy-start.2 = (bf16[1,1,360,1536]{3,2,1,0:T(8,128)(2,1)S(1)}, bf16[1,1,360,1536]{3,2,1,0:T(8,128)(2,1)}, u32[]{:S(2)}) copy-start(bf16[1,1,360,1536]{3,2,1,0:T(8,128)(2,1)} %param.14) | copy-start | bytes 3317764
  7.2 73.2 %all-gather.6.cloned.1.call-start = ((), (), s32[]{:S(2)}) async-start(), calls=%async_computation.5 | async-start | bytes 5308416 | tf_op jit(solution)/shard_map/all_gather | solution.py:72
  7.3 17.9 %collective-permute-start.8 = (bf16[1,72,4096]{2,1,0:T(8,128)(2,1)}, bf16[1,72,4096]{2,1,0:T(8,128)(2,1)S(1)}, u32[]{:S(2)}, u32[]{:S(2)}) collective-permute-start(bf16[1,72,4096]{2,1,0:T(8,128)(2,1)} %param.12), channel_id=1, source_target_pairs={{0,8},{8,16},{16,24},{1,9},{9,17},{17,25},{2,10},{10,18},{18,26},{... | collective-permute-start | bytes 1769480 | tf_op jit(solution)/shard_map/ppermute | solution.py:12
  27.1 135.0 %reduce-scatter.5.cloned.1.call-start = ((), (), s32[]{:S(2)}) async-start(), calls=%async_computation.4 | async-start | bytes 5308416 | tf_op jit(solution)/shard_map/reduce_scatter | solution.py:107
  27.3 4.9 %collective-permute-start.1 = (f32[72,16]{0,1:T(8,128)S(1)}, f32[72,16]{0,1:T(8,128)S(1)}, u32[]{:S(2)}, u32[]{:S(2)}) collective-permute-start(f32[72,16]{0,1:T(8,128)S(1)} %pad_maximum_fusion), channel_id=1, source_target_pairs={{0,1},{1,2},{2,3},{3,4},{4,5},{5,6},{6,7},{7,0},{8,9},{9,10},{10,1... | collective-permute-start | bytes 13832 | tf_op jit(solution)/shard_map/ppermute | solution.py:51
  32.2 4.9 %collective-permute-start.2 = (f32[72,16]{0,1:T(8,128)S(1)}, f32[72,16]{0,1:T(8,128)S(1)}, u32[]{:S(2)}, u32[]{:S(2)}) collective-permute-start(f32[72,16]{0,1:T(8,128)S(1)} %collective-permute-done.1), channel_id=1, source_target_pairs={{0,1},{1,2},{2,3},{3,4},{4,5},{5,6},{6,7},{7,0},{8,9},{9,10},{10,1... | collective-permute-start | bytes 13832 | tf_op jit(solution)/shard_map/ppermute | solution.py:51
  37.1 5.0 %collective-permute-start.3 = (f32[72,16]{0,1:T(8,128)S(1)}, f32[72,16]{0,1:T(8,128)S(1)}, u32[]{:S(2)}, u32[]{:S(2)}) collective-permute-start(f32[72,16]{0,1:T(8,128)S(1)} %collective-permute-done.2), channel_id=1, source_target_pairs={{0,1},{1,2},{2,3},{3,4},{4,5},{5,6},{6,7},{7,0},{8,9},{9,10},{10,1... | collective-permute-start | bytes 13832 | tf_op jit(solution)/shard_map/ppermute | solution.py:51
  42.1 5.0 %collective-permute-start.4 = (f32[72,16]{0,1:T(8,128)S(1)}, f32[72,16]{0,1:T(8,128)S(1)}, u32[]{:S(2)}, u32[]{:S(2)}) collective-permute-start(f32[72,16]{0,1:T(8,128)S(1)} %collective-permute-done.3), channel_id=1, source_target_pairs={{0,1},{1,2},{2,3},{3,4},{4,5},{5,6},{6,7},{7,0},{8,9},{9,10},{10,1... | collective-permute-start | bytes 13832 | tf_op jit(solution)/shard_map/ppermute | solution.py:51
  47.2 5.1 %collective-permute-start.5 = (f32[72,16]{0,1:T(8,128)S(1)}, f32[72,16]{0,1:T(8,128)S(1)}, u32[]{:S(2)}, u32[]{:S(2)}) collective-permute-start(f32[72,16]{0,1:T(8,128)S(1)} %collective-permute-done.4), channel_id=1, source_target_pairs={{0,1},{1,2},{2,3},{3,4},{4,5},{5,6},{6,7},{7,0},{8,9},{9,10},{10,1... | collective-permute-start | bytes 13832 | tf_op jit(solution)/shard_map/ppermute | solution.py:51
  52.2 5.1 %collective-permute-start.6 = (f32[72,16]{0,1:T(8,128)S(1)}, f32[72,16]{0,1:T(8,128)S(1)}, u32[]{:S(2)}, u32[]{:S(2)}) collective-permute-start(f32[72,16]{0,1:T(8,128)S(1)} %collective-permute-done.5), channel_id=1, source_target_pairs={{0,1},{1,2},{2,3},{3,4},{4,5},{5,6},{6,7},{7,0},{8,9},{9,10},{10,1... | collective-permute-start | bytes 13832 | tf_op jit(solution)/shard_map/ppermute | solution.py:51
  57.3 5.1 %collective-permute-start.7 = (f32[72,16]{0,1:T(8,128)S(1)}, f32[72,16]{0,1:T(8,128)S(1)}, u32[]{:S(2)}, u32[]{:S(2)}) collective-permute-start(f32[72,16]{0,1:T(8,128)S(1)} %collective-permute-done.6), channel_id=1, source_target_pairs={{0,1},{1,2},{2,3},{3,4},{4,5},{5,6},{6,7},{7,0},{8,9},{9,10},{10,1... | collective-permute-start | bytes 13832 | tf_op jit(solution)/shard_map/ppermute | solution.py:51
  108.2 1.1 copy-start.3
  108.2 53.9 %copy-start.1 = (bf16[1,72,4096]{2,1,0:T(8,128)(2,1)S(1)}, bf16[1,72,4096]{2,1,0:T(8,128)(2,1)}, u32[]{:S(2)}) copy-start(bf16[1,72,4096]{2,1,0:T(8,128)(2,1)} %param.13) | copy-start | bytes 1769476
  108.2 53.9 %copy-start.4 = (f32[1,4096]{1,0:T(1,128)S(1)}, f32[1,4096]{1,0:T(1,128)}, u32[]{:S(2)}) copy-start(f32[1,4096]{1,0:T(1,128)} %param.15) | copy-start | bytes 49156
  108.2 55.4 %copy-start = (bf16[1,72,4096]{2,1,0:T(8,128)(2,1)S(1)}, bf16[1,72,4096]{2,1,0:T(8,128)(2,1)}, u32[]{:S(2)}) copy-start(bf16[1,72,4096]{2,1,0:T(8,128)(2,1)} %broadcast_select_fusion) | copy-start | bytes 1769476
  108.2 108.2 %all-gather.4.cloned.1.call-start = ((), (), s32[]{:S(2)}) async-start(), calls=%async_computation.2 | async-start | bytes 5308416 | tf_op jit(solution)/shard_map/all_gather | solution.py:71
  109.2 16.3 %collective-permute-start = (bf16[1,72,4096]{2,1,0:T(8,128)(2,1)S(1)}, bf16[1,72,4096]{2,1,0:T(8,128)(2,1)S(1)}, u32[]{:S(2)}, u32[]{:S(2)}) collective-permute-start(bf16[1,72,4096]{2,1,0:T(8,128)(2,1)S(1)} %copy-done.3), channel_id=1, source_target_pairs={{0,8},{8,16},{16,24},{1,9},{9,17},{17,25},{2,10},{10,18},{18,26},{... | collective-permute-start | bytes 1769480 | tf_op jit(solution)/shard_map/ppermute | solution.py:12
  166.3 124.0 %reduce-scatter.3.cloned.1.call-start = ((), (), s32[]{:S(2)}) async-start(), calls=%async_computation.3 | async-start | bytes 5308416 | tf_op jit(solution)/shard_map/reduce_scatter | solution.py:79
Sparse Core Ops, SparseCore 0:
  27.2 53.1 all-gather.5
  108.3 53.7 reduce-scatter.4
  166.4 50.0 all-gather.3
  236.5 53.7 reduce-scatter.2
